TPU v7x, 32 devices: a whole 2x2x4 slice. The times are simulated.
32 devices in a mesh: tile: 4 (over x, core), frame: 8 (over z, y).
Axes of the slice: x: 2, y: 2, z: 4, core: 2. Of those that a mesh axis runs over, the one named last changes fastest.
Arguments:
- queries: bfloat16 [8192, 1536], P(('tile', 'frame')), may hold values from -5 to 5
- keys: bfloat16 [8192, 1536], P(('tile', 'frame')), may hold values from -5 to 5
- values: bfloat16 [8192, 1536], P(('tile', 'frame')), may hold values from -6 to 6
- block_lists: int32 [64, 26], replicated, may hold values from -1 to 63, as said below
Outputs:
- attended: bfloat16 [8192, 1536], P(('tile', 'frame'))
Inputs may be any that keep to these rules, and one draw needn't show every extreme that they name: `block_lists`: block b belongs to spatial tile (b // 2) // 8 and frame group (b // 2) % 8. Row b lists first, without repeats, the key blocks that query block b attends to, then -1 to its end. Every listed block lies at a squared distance of at most 4 from block b in (tile, frame group), and all blocks of b's own tile and frame group are listed.
All inputs are finite; a program needn't handle non-finite values.
Results may differ from a plain program's by a relative error of at most 0.004.
Values may be sent and summed in bfloat16 or wider, within the bound.
A program may use at most 128 MiB of HBM per device.

v0:
```python
import functools
import math

import jax
import jax.numpy as jnp
from jax import lax
from jax.experimental import pallas as pl
from jax.experimental.pallas import tpu as pltpu
from jax.sharding import PartitionSpec as P

HEADS = 12
DH = 128
BLK = 128
CHUNKS = 3
PER = HEADS // CHUNKS
HALF = PER * DH
NEGATIVE = -1e30
SCALE = math.log2(math.e) / math.sqrt(DH)

SELF, PART, NEAR, ZA, ZB, X1, X2, X3, DIAG, PNEAR, PDIAG, XNEAR, XDIAG = range(13)
SLOTS = 13
STAGES = (
    (0, (SELF,)),
    (1, (PART, NEAR, ZA, ZB, X1, X2)),
    (2, (DIAG, X3, PNEAR, XNEAR)),
    (3, (PDIAG, XDIAG)),
)
RELAYED = (NEAR, ZB, X1, DIAG)
DIAG_Z, DIAG_Y = (0,), (1, 2)
XNEAR_X, XNEAR_Y = (0, 1), (2,)


def geometry():
    tiles, groups = lax.axis_size("tile"), lax.axis_size("frame")
    t, g = lax.axis_index("tile"), lax.axis_index("frame")
    f = 2 * lax.rem(t, 2) - 1
    d = 2 * lax.rem(g, 2) - 1
    offsets = (
        (0, 0), (-f, 0), (0, -d), (0, 2 * d), (0, -2 * d), (f, 0), (2 * f, 0), (-2 * f, 0),
        (0, d), (-f, -d), (-f, d), (f, -d), (f, d),
    )
    return tiles, groups, t, g, f, d, offsets


def kernel(q_hbm, k_ref, v_ref, lists_ref, o_ref, q_ref, bias, buf, acc, top, total, q_sem, own_sem, send_sem, recv_sem):
    tiles, groups, t, g, f, d, offsets = geometry()

    def inside(dt, dg):
        a, b = t + dt, g + dg
        return (a >= 0) & (a < tiles) & (b >= 0) & (b < groups)

    valid = [inside(*offset) for offset in offsets]
    peers = ((-f, 0), (0, -d), (0, 2), (0, -2), (f, 0), (2, 0), (-2, 0))

    def own_copy(j, which):
        ref = (k_ref, v_ref)[which]
        return pltpu.make_async_copy(
            ref.at[:, pl.ds(j * HALF, HALF)],
            buf.at[SELF, j, :, pl.ds(which * HALF, HALF)],
            own_sem.at[j, which],
        )

    for j in range(CHUNKS):
        for which in range(2):
            own_copy(j, which).start()
    q_copy = pltpu.make_async_copy(q_hbm, q_ref, q_sem)
    q_copy.start()

    barrier = pltpu.get_barrier_semaphore()
    for dt, dg in peers:
        @pl.when(inside(dt, dg))
        def _():
            pl.semaphore_signal(
                barrier, inc=1, device_id=(t + dt, g + dg), device_id_type=pl.DeviceIdType.MESH
            )
    pl.semaphore_wait(barrier, sum(inside(*peer).astype(jnp.int32) for peer in peers))

    every = tuple(range(CHUNKS))
    moves = (
        (SELF, NEAR, (0, -d), every),
        (SELF, ZA, (0, -2 * d), every),
        (SELF, ZB, (0, 2 * d), every),
        (SELF, X1, (f, 0), every),
        (SELF, X2, (-2 * f, 0), every),
        (SELF, PART, (-f, 0), every),
        (NEAR, DIAG, (0, -2 * d), DIAG_Z),
        (ZB, DIAG, (0, -d), DIAG_Y),
        (NEAR, XNEAR, (f, 0), XNEAR_X),
        (X1, XNEAR, (0, -d), XNEAR_Y),
        (NEAR, PNEAR, (-f, 0), every),
        (X1, X3, (-f, 0), every),
        (DIAG, XDIAG, (f, 0), every),
        (DIAG, PDIAG, (-f, 0), every),
    )

    def among(j, chunks):
        hit = j == chunks[0]
        for other in chunks[1:]:
            hit = hit | (j == other)
        return hit

    def each_move(j, sources, act):
        for index, (source, slot, place, chunks) in enumerate(moves):
            if source not in sources:
                continue
            where = inside(*place) & valid[source]
            if len(chunks) < CHUNKS:
                where = where & among(j, chunks)

            @pl.when(where)
            def _():
                act(
                    pltpu.make_async_remote_copy(
                        src_ref=buf.at[source, j],
                        dst_ref=buf.at[slot, j],
                        send_sem=send_sem.at[index, j],
                        recv_sem=recv_sem.at[slot, j],
                        device_id=(t + place[0], g + place[1]),
                        device_id_type=pl.DeviceIdType.MESH,
                    )
                )

    def arrived(slot, j):
        pltpu.make_async_copy(buf.at[slot, j], buf.at[slot, j], recv_sem.at[slot, j]).wait()

    def finish(j):
        for hh in range(PER):
            head = j * PER + hh
            cols = pl.ds(pl.multiple_of(head * DH, DH), DH)
            denom = jnp.sum(total[head], axis=1, keepdims=True)
            o_ref[:, cols] = (acc[:, cols] / denom).astype(jnp.bfloat16)

    def mask_rows():
        lists = lists_ref[...]
        block = lax.broadcasted_iota(jnp.int32, lists.shape, 1)
        second = lax.broadcasted_iota(jnp.int32, (1, 2 * BLK), 1) // BLK
        for half in range(2):
            mine = 2 * (t * groups + g) + half
            listed = jnp.sum(jnp.where(block == mine, lists, 0), axis=1, keepdims=True)
            for slot, (dt, dg) in enumerate(offsets):
                ids = 2 * ((t + dt) * groups + g + dg) + second
                hit = jnp.max(jnp.where(listed == ids, 1, 0), axis=0, keepdims=True)
                bias[2 * slot + half:2 * slot + half + 1, :] = jnp.where(hit > 0, 0.0, NEGATIVE)

    def compute(slot, j):
        upper = bias[2 * slot:2 * slot + 1, :]
        lower = bias[2 * slot + 1:2 * slot + 2, :]
        for hh in range(PER):
            head = j * PER + hh
            cols = pl.ds(pl.multiple_of(head * DH, DH), DH)
            k = buf[slot, j, :, hh * DH:(hh + 1) * DH]
            v = buf[slot, j, :, HALF + hh * DH:HALF + (hh + 1) * DH]
            s = lax.dot_general(
                q_ref[:, cols], k, (((1,), (1,)), ((), ())), preferred_element_type=jnp.float32
            )
            s = jnp.concatenate([s[:BLK] * SCALE + upper, s[BLK:] * SCALE + lower], axis=0)
            peak = jnp.max(s, axis=1, keepdims=True)
            if slot == SELF:
                new = jnp.broadcast_to(peak, (2 * BLK, DH))
            else:
                old = top[head]
                new = jnp.maximum(old, peak)
            p = jnp.exp2(s - jnp.concatenate([new, new], axis=1))
            part = p[:, :DH] + p[:, DH:]
            mixed = jnp.dot(p.astype(jnp.bfloat16), v, preferred_element_type=jnp.float32)
            if slot != SELF:
                rescale = jnp.exp2(old - new)
                part = part + total[head] * rescale
                mixed = mixed + acc[:, cols] * rescale
            top[head] = new
            total[head] = part
            acc[:, cols] = mixed

    def step(tick, carry):
        @pl.when(tick < CHUNKS)
        def _():
            own_copy(tick, 0).wait()
            own_copy(tick, 1).wait()
            each_move(tick, (SELF,), lambda copy: copy.start())

        @pl.when(tick == 0)
        def _():
            mask_rows()
            q_copy.wait()

        for lag, members in STAGES:
            j = tick - lag

            @pl.when((j >= 0) & (j < CHUNKS))
            def _():
                for slot in members:
                    if slot in RELAYED:
                        @pl.when(valid[slot])
                        def _():
                            arrived(slot, j)
                        each_move(j, (slot,), lambda copy: copy.start())
        for lag, members in STAGES:
            j = tick - lag

            @pl.when((j >= 0) & (j < CHUNKS))
            def _():
                for slot in members:
                    @pl.when(valid[slot])
                    def _():
                        if slot != SELF and slot not in RELAYED:
                            arrived(slot, j)
                        compute(slot, j)
                if members == STAGES[-1][1]:
                    finish(j)
        return carry
    lax.fori_loop(0, CHUNKS + STAGES[-1][0], step, 0)

    def drain(j, carry):
        each_move(j, tuple(range(SLOTS)), lambda copy: copy.wait_send())
        return carry
    lax.fori_loop(0, CHUNKS, drain, 0)


def shards(queries, keys, values, block_lists):
    rows, width = queries.shape
    vmem = pl.BlockSpec(memory_space=pltpu.VMEM)
    return pl.pallas_call(
        kernel,
        out_shape=jax.ShapeDtypeStruct((rows, width), jnp.bfloat16),
        in_specs=[
            pl.BlockSpec(memory_space=pl.ANY),
            pl.BlockSpec(memory_space=pl.ANY),
            pl.BlockSpec(memory_space=pl.ANY),
            vmem,
        ],
        out_specs=vmem,
        scratch_shapes=[
            pltpu.VMEM((rows, width), jnp.bfloat16),
            pltpu.VMEM((2 * SLOTS, rows), jnp.float32),
            pltpu.VMEM((SLOTS, CHUNKS, rows, 2 * HALF), jnp.bfloat16),
            pltpu.VMEM((rows, width), jnp.float32),
            pltpu.VMEM((HEADS, rows, DH), jnp.float32),
            pltpu.VMEM((HEADS, rows, DH), jnp.float32),
            pltpu.SemaphoreType.DMA,
            pltpu.SemaphoreType.DMA((CHUNKS, 2)),
            pltpu.SemaphoreType.DMA((14, CHUNKS)),
            pltpu.SemaphoreType.DMA((SLOTS, CHUNKS)),
        ],
        compiler_params=pltpu.CompilerParams(
            collective_id=0, has_side_effects=True, vmem_limit_bytes=67043328
        ),
    )(queries, keys, values, block_lists.T)


def solution(mesh):
    placed = P(("tile", "frame"), None)
    return jax.shard_map(
        shards, mesh=mesh, in_specs=(placed, placed, placed, P()), out_specs=placed, check_vma=False
    )
```

profile of v0, /device:TPU:17, one launch (start us, length us, event | category | flops | bytes accessed | tf_op | source)
XLA Modules:
  0.0 75.1 jit_solution(5285921935980666528)
XLA Ops:
  0.0 73.1 %shard_map.46 = bf16[256,1536]{1,0:T(8,128)(2,1)} custom-call(bf16[256,1536]{1,0:T(8,128)(2,1)} %q_hbm.1, bf16[256,1536]{1,0:T(8,128)(2,1)} %k_ref.1, bf16[256,1536]{1,0:T(8,128)(2,1)} %v_ref.1, s32[26,64]{1,0:T(8,128)} %bitcast.1), custom_call_target="tpu_custom_call" | custom-call | tf_op jit(solution)/shard_map/pallas_call | solution.py:222
  73.1 2.1 %copy.6 = bf16[256,1536]{1,0:T(8,128)(2,1)} copy(bf16[256,1536]{1,0:T(8,128)(2,1)} %shard_map.46) | data formatting | bytes 1572864
where the time goes:
time: 75.4 us; the launch traced here: 75.1 us
  Pallas kernels  73.1 us (97%)
  local copies, waits for them, and re-layouts  2.06 us (3%)
    pallas_call x1, Pallas kernels, shards(): pl.pallas_call(kernel, out_shape=jax.ShapeDtypeStruct((rows, width), jnp....  73.1 us
    unnamed x1, local copies, waits for them, and re-layouts  2.06 us

commit v1 on v0

v1 whole, which is shorter than its diff:
```python
import math

import jax
import jax.numpy as jnp
from jax import lax
from jax.experimental import pallas as pl
from jax.experimental.pallas import tpu as pltpu
from jax.sharding import PartitionSpec as P

HEADS = 12
DH = 128
BLK = 128
PER = 2
CHUNKS = HEADS // PER
HALF = PER * DH
NEGATIVE = -1e30
FLOOR = -1e29
SCALE = math.log2(math.e) / math.sqrt(DH)

SELF, PART, X1, X2, X3, ZA, ZB, PZB, XZB = range(9)
SLOTS = 9
OWN = (SELF, PART, X1, X2, X3, ZA, ZB)
GUEST = (SELF, PART, X1, ZB, PZB, XZB)
BIAS_ROW = {(0, slot): 2 * n for n, slot in enumerate(OWN)}
BIAS_ROW.update({(1, slot): 2 * (len(OWN) + n) for n, slot in enumerate(GUEST)})
BIAS_ROWS = 32
AHEAD = 1
LAG_X = 2
LAG_OUT = 4
VIA_X = tuple(range(0, CHUNKS, 2))
VIA_Z = tuple(range(1, CHUNKS, 2))


def geometry():
    tiles, groups = lax.axis_size("tile"), lax.axis_size("frame")
    t, g = lax.axis_index("tile"), lax.axis_index("frame")
    f = 2 * lax.rem(t, 2) - 1
    d = 2 * lax.rem(g, 2) - 1
    offsets = (
        (0, 0), (-f, 0), (f, 0), (2 * f, 0), (-2 * f, 0), (0, 2 * d), (0, -2 * d), (-f, -2 * d), (f, -2 * d),
    )
    return tiles, groups, t, g, f, d, offsets


def kernel(
    q_hbm, k_hbm, v_hbm, lists_ref, o_ref,
    qbuf, bias, buf, acc, top, total, guest_out, guest_stat, back_out, back_stat,
    own_sem, send_sem, recv_sem, q_send, q_recv, out_send, out_recv, stat_send, stat_recv,
):
    tiles, groups, t, g, f, d, offsets = geometry()

    def inside(dt, dg):
        a, b = t + dt, g + dg
        return (a >= 0) & (a < tiles) & (b >= 0) & (b < groups)

    valid = [inside(*offset) for offset in offsets]
    peers = ((-f, 0), (0, -d), (0, 2), (0, -2), (f, 0), (2, 0), (-2, 0))

    def own_copy(j, which):
        ref = (k_hbm, v_hbm, q_hbm)[which]
        place = qbuf.at[0, j] if which == 2 else buf.at[SELF, j, :, pl.ds(which * HALF, HALF)]
        return pltpu.make_async_copy(ref.at[:, pl.ds(j * HALF, HALF)], place, own_sem.at[j, which])

    for j in range(CHUNKS):
        for which in range(3):
            own_copy(j, which).start()

    barrier = pltpu.get_barrier_semaphore()
    for dt, dg in peers:
        @pl.when(inside(dt, dg))
        def _():
            pl.semaphore_signal(
                barrier, inc=1, device_id=(t + dt, g + dg), device_id_type=pl.DeviceIdType.MESH
            )
    pl.semaphore_wait(barrier, sum(inside(*peer).astype(jnp.int32) for peer in peers))

    every = tuple(range(CHUNKS))
    moves = (
        (SELF, X1, (f, 0), every),
        (SELF, ZB, (0, 2 * d), every),
        (SELF, PART, (-f, 0), every),
        (SELF, X2, (-2 * f, 0), every),
        (SELF, ZA, (0, -2 * d), every),
        (X1, X3, (-f, 0), every),
        (X1, XZB, (0, 2 * d), VIA_Z),
        (ZB, PZB, (-f, 0), every),
        (ZB, XZB, (f, 0), VIA_X),
    )

    def among(j, chunks):
        hit = j == chunks[0]
        for other in chunks[1:]:
            hit = hit | (j == other)
        return hit

    def each_move(j, sources, act):
        for index, (source, slot, place, chunks) in enumerate(moves):
            if source not in sources or not chunks:
                continue
            where = inside(*place) & valid[source]
            if len(chunks) < CHUNKS:
                where = where & among(j, chunks)

            @pl.when(where)
            def _():
                act(
                    pltpu.make_async_remote_copy(
                        src_ref=buf.at[source, j],
                        dst_ref=buf.at[slot, j],
                        send_sem=send_sem.at[index, j],
                        recv_sem=recv_sem.at[slot, j],
                        device_id=(t + place[0], g + place[1]),
                        device_id_type=pl.DeviceIdType.MESH,
                    )
                )

    def to_pair(src, dst, send, recv):
        return pltpu.make_async_remote_copy(
            src_ref=src, dst_ref=dst, send_sem=send, recv_sem=recv,
            device_id=(t, g - d), device_id_type=pl.DeviceIdType.MESH,
        )

    def q_move(j):
        return to_pair(qbuf.at[0, j], qbuf.at[1, j], q_send.at[j], q_recv.at[j])

    def out_move(j):
        return to_pair(guest_out.at[j], back_out.at[j], out_send.at[j], out_recv.at[j])

    def stat_move(j):
        return to_pair(guest_stat.at[j], back_stat.at[j], stat_send.at[j], stat_recv.at[j])

    def arrived(slot, j):
        pltpu.make_async_copy(buf.at[slot, j], buf.at[slot, j], recv_sem.at[slot, j]).wait()

    def mask_rows():
        lists = lists_ref[...]
        block = lax.broadcasted_iota(jnp.int32, lists.shape, 1)
        first = lax.broadcasted_iota(jnp.int32, (lists.shape[0], 2 * BLK), 1) < BLK
        for who, slots, base in ((0, OWN, 2 * (t * groups + g)), (1, GUEST, 2 * (t * groups + g - d))):
            upper = jnp.sum(jnp.where(block == base, lists, 0), axis=1, keepdims=True)
            lower = jnp.sum(jnp.where(block == base + 1, lists, 0), axis=1, keepdims=True)
            listed = jnp.where(first, upper, lower)
            for slot in slots:
                dt, dg = offsets[slot]
                for half in range(2):
                    name = 2 * ((t + dt) * groups + g + dg) + half
                    hit = jnp.max(jnp.where(listed == name, 1, 0), axis=0, keepdims=True)
                    row = BIAS_ROW[who, slot] + half
                    bias[row:row + 1, :] = jnp.where(hit > 0, 0.0, NEGATIVE)

    def compute(slot, j, users):
        for hh in range(PER):
            k = buf[slot, j, :, hh * DH:(hh + 1) * DH]
            v = buf[slot, j, :, HALF + hh * DH:HALF + (hh + 1) * DH]
            head = j * PER + hh
            for who in users:
                row = BIAS_ROW[who, slot]
                b0, b1 = bias[row:row + 1, :], bias[row + 1:row + 2, :]
                s = lax.dot_general(
                    k, qbuf[who, j, :, hh * DH:(hh + 1) * DH], (((1,), (1,)), ((), ())),
                    preferred_element_type=jnp.float32,
                )
                s0, s1 = s[:BLK], s[BLK:]
                peak = jnp.maximum(
                    jnp.max(s0, axis=0, keepdims=True) * SCALE + b0,
                    jnp.max(s1, axis=0, keepdims=True) * SCALE + b1,
                )
                if slot == SELF:
                    new = jnp.maximum(peak, FLOOR)
                else:
                    old = top[who, head, 0:1, :]
                    new = jnp.maximum(old, peak)
                p = jnp.concatenate(
                    [jnp.exp2(s0 * SCALE - (new - b0)), jnp.exp2(s1 * SCALE - (new - b1))], axis=0
                )
                part = jnp.sum(p.reshape(2 * BLK // 8, 8, 2 * BLK), axis=0)
                mixed = lax.dot_general(
                    v, p.astype(jnp.bfloat16), (((0,), (0,)), ((), ())), preferred_element_type=jnp.float32
                )
                if slot != SELF:
                    rescale = jnp.exp2(old - new)
                    part = part + total[who, head] * rescale
                    mixed = mixed + acc[who, head] * rescale
                top[who, head, 0:1, :] = new
                total[who, head] = part
                acc[who, head] = mixed

    def pack_guest(j):
        for hh in range(PER):
            head = j * PER + hh
            guest_out[j, hh * DH:(hh + 1) * DH, :] = acc[1, head].astype(jnp.bfloat16)
            guest_stat[j, 2 * hh:2 * hh + 1, :] = top[1, head, 0:1, :]
            guest_stat[j, 2 * hh + 1:2 * hh + 2, :] = jnp.sum(total[1, head], axis=0, keepdims=True)

    def finish(j):
        for hh in range(PER):
            head = j * PER + hh
            m1, m2 = top[0, head, 0:1, :], back_stat[j, 2 * hh:2 * hh + 1, :]
            m = jnp.maximum(m1, m2)
            e1, e2 = jnp.exp2(m1 - m), jnp.exp2(m2 - m)
            l1 = jnp.sum(total[0, head], axis=0, keepdims=True)
            denom = l1 * e1 + back_stat[j, 2 * hh + 1:2 * hh + 2, :] * e2
            other = back_out[j, hh * DH:(hh + 1) * DH, :].astype(jnp.float32)
            mixed = acc[0, head] * (e1 / denom) + other * (e2 / denom)
            cols = pl.ds(pl.multiple_of(head * DH, DH), DH)
            o_ref[:, cols] = mixed.T.astype(jnp.bfloat16)

    def launch(j):
        own_copy(j, 0).wait()
        own_copy(j, 1).wait()
        each_move(j, (SELF,), lambda copy: copy.start())

    def when_valid(slot, j, users, wait=True):
        @pl.when(valid[slot])
        def _():
            if wait:
                arrived(slot, j)
            compute(slot, j, users)

    for j in range(AHEAD):
        launch(j)

    def send_q(j, carry):
        own_copy(j, 2).wait()
        q_move(j).start()
        return carry
    lax.fori_loop(0, CHUNKS, send_q, 0)
    mask_rows()

    def step(tick, carry):
        @pl.when(tick + AHEAD < CHUNKS)
        def _():
            launch(tick + AHEAD)

        @pl.when(tick < CHUNKS)
        def _():
            compute(SELF, tick, (0,))
            q_move(tick).wait_recv()
            compute(SELF, tick, (1,))
            when_valid(PART, tick, (0, 1))
            for slot in (X1, ZB):
                @pl.when(valid[slot])
                def _():
                    arrived(slot, tick)
                each_move(tick, (slot,), lambda copy: copy.start())
            for slot in (X1, ZB):
                when_valid(slot, tick, (0, 1), wait=False)

        j = tick - LAG_X

        @pl.when((j >= 0) & (j < CHUNKS))
        def _():
            when_valid(PZB, j, (1,))
            when_valid(XZB, j, (1,))
            pack_guest(j)

        @pl.when(tick < CHUNKS)
        def _():
            when_valid(X2, tick, (0,))
            when_valid(ZA, tick, (0,))

        @pl.when((j >= 0) & (j < CHUNKS))
        def _():
            when_valid(X3, j, (0,))
            out_move(j).start()
            stat_move(j).start()

        last = tick - LAG_OUT

        @pl.when((last >= 0) & (last < CHUNKS))
        def _():
            out_move(last).wait_recv()
            stat_move(last).wait_recv()
            finish(last)
        return carry
    lax.fori_loop(0, CHUNKS + LAG_OUT, step, 0)

    def drain(j, carry):
        each_move(j, tuple(range(SLOTS)), lambda copy: copy.wait_send())
        q_move(j).wait_send()
        out_move(j).wait_send()
        stat_move(j).wait_send()
        return carry
    lax.fori_loop(0, CHUNKS, drain, 0)


def shards(queries, keys, values, block_lists):
    rows, width = queries.shape
    vmem = pl.BlockSpec(memory_space=pltpu.VMEM)
    anywhere = pl.BlockSpec(memory_space=pl.ANY)
    return pl.pallas_call(
        kernel,
        out_shape=jax.ShapeDtypeStruct((rows, width), jnp.bfloat16),
        in_specs=[anywhere, anywhere, anywhere, vmem],
        out_specs=vmem,
        scratch_shapes=[
            pltpu.VMEM((2, CHUNKS, rows, HALF), jnp.bfloat16),
            pltpu.VMEM((BIAS_ROWS, rows), jnp.float32),
            pltpu.VMEM((SLOTS, CHUNKS, rows, 2 * HALF), jnp.bfloat16),
            pltpu.VMEM((2, HEADS, DH, rows), jnp.float32),
            pltpu.VMEM((2, HEADS, 8, rows), jnp.float32),
            pltpu.VMEM((2, HEADS, 8, rows), jnp.float32),
            pltpu.VMEM((CHUNKS, HALF, rows), jnp.bfloat16),
            pltpu.VMEM((CHUNKS, 8, rows), jnp.float32),
            pltpu.VMEM((CHUNKS, HALF, rows), jnp.bfloat16),
            pltpu.VMEM((CHUNKS, 8, rows), jnp.float32),
            pltpu.SemaphoreType.DMA((CHUNKS, 3)),
            pltpu.SemaphoreType.DMA((9, CHUNKS)),
            pltpu.SemaphoreType.DMA((SLOTS, CHUNKS)),
            pltpu.SemaphoreType.DMA((CHUNKS,)),
            pltpu.SemaphoreType.DMA((CHUNKS,)),
            pltpu.SemaphoreType.DMA((CHUNKS,)),
            pltpu.SemaphoreType.DMA((CHUNKS,)),
            pltpu.SemaphoreType.DMA((CHUNKS,)),
            pltpu.SemaphoreType.DMA((CHUNKS,)),
        ],
        compiler_params=pltpu.CompilerParams(
            collective_id=0, has_side_effects=True, vmem_limit_bytes=67043328
        ),
    )(queries, keys, values, block_lists.T)


def solution(mesh):
    placed = P(("tile", "frame"), None)
    return jax.shard_map(
        shards, mesh=mesh, in_specs=(placed, placed, placed, P()), out_specs=placed, check_vma=False
    )
```

time: 75.4 us -> 71.3 us (0.946)
  Pallas kernels: 73.1 us -> 69 us
    pallas_call x1, Pallas kernels: 73.1 us -> 69 us  [shards(): pl.pallas_call(kernel, out_shape=jax.ShapeDtypeStruct((rows, width), jnp....]
where the time goes in v1:
time: 71.3 us; the launch traced here: 71.1 us
  Pallas kernels  69 us (97%)
  local copies, waits for them, and re-layouts  2.06 us (3%)
    pallas_call x1, Pallas kernels, shards(): pl.pallas_call(kernel, out_shape=jax.ShapeDtypeStruct((rows, width), jnp....  69 us
    unnamed x1, local copies, waits for them, and re-layouts  2.06 us

profile of v1, /device:TPU:17, one launch (start us, length us, event | category | flops | bytes accessed | tf_op | source)
XLA Modules:
  0.0 71.1 jit_solution(3042233646822571649)
XLA Ops:
  0.0 69.0 %shard_map.46 = bf16[256,1536]{1,0:T(8,128)(2,1)} custom-call(bf16[256,1536]{1,0:T(8,128)(2,1)} %q_hbm.1, bf16[256,1536]{1,0:T(8,128)(2,1)} %k_hbm.1, bf16[256,1536]{1,0:T(8,128)(2,1)} %v_hbm.1, s32[26,64]{1,0:T(8,128)} %bitcast.1), custom_call_target="tpu_custom_call" | custom-call | tf_op jit(solution)/shard_map/pallas_call | solution.py:291
  69.0 2.1 %copy.6 = bf16[256,1536]{1,0:T(8,128)(2,1)} copy(bf16[256,1536]{1,0:T(8,128)(2,1)} %shard_map.46) | data formatting | bytes 1572864

commit v2 on v1

--- a/solution.py
+++ b/solution.py
@@ -14,7 +14,6 @@
 CHUNKS = HEADS // PER
 HALF = PER * DH
 NEGATIVE = -1e30
-FLOOR = -1e29
 SCALE = math.log2(math.e) / math.sqrt(DH)
 
 SELF, PART, X1, X2, X3, ZA, ZB, PZB, XZB = range(9)
@@ -135,16 +134,14 @@
     def mask_rows():
         lists = lists_ref[...]
         block = lax.broadcasted_iota(jnp.int32, lists.shape, 1)
-        first = lax.broadcasted_iota(jnp.int32, (lists.shape[0], 2 * BLK), 1) < BLK
+        second = lax.broadcasted_iota(jnp.int32, (1, 2 * BLK), 1) // BLK
         for who, slots, base in ((0, OWN, 2 * (t * groups + g)), (1, GUEST, 2 * (t * groups + g - d))):
-            upper = jnp.sum(jnp.where(block == base, lists, 0), axis=1, keepdims=True)
-            lower = jnp.sum(jnp.where(block == base + 1, lists, 0), axis=1, keepdims=True)
-            listed = jnp.where(first, upper, lower)
-            for slot in slots:
-                dt, dg = offsets[slot]
-                for half in range(2):
-                    name = 2 * ((t + dt) * groups + g + dg) + half
-                    hit = jnp.max(jnp.where(listed == name, 1, 0), axis=0, keepdims=True)
+            for half in range(2):
+                listed = jnp.sum(jnp.where(block == base + half, lists, 0), axis=1, keepdims=True)
+                for slot in slots:
+                    dt, dg = offsets[slot]
+                    names = 2 * ((t + dt) * groups + g + dg) + second
+                    hit = jnp.max(jnp.where(listed == names, 1, 0), axis=0, keepdims=True)
                     row = BIAS_ROW[who, slot] + half
                     bias[row:row + 1, :] = jnp.where(hit > 0, 0.0, NEGATIVE)
 
@@ -155,55 +152,53 @@
             head = j * PER + hh
             for who in users:
                 row = BIAS_ROW[who, slot]
-                b0, b1 = bias[row:row + 1, :], bias[row + 1:row + 2, :]
                 s = lax.dot_general(
-                    k, qbuf[who, j, :, hh * DH:(hh + 1) * DH], (((1,), (1,)), ((), ())),
+                    qbuf[who, j, :, hh * DH:(hh + 1) * DH], k, (((1,), (1,)), ((), ())),
                     preferred_element_type=jnp.float32,
                 )
-                s0, s1 = s[:BLK], s[BLK:]
-                peak = jnp.maximum(
-                    jnp.max(s0, axis=0, keepdims=True) * SCALE + b0,
-                    jnp.max(s1, axis=0, keepdims=True) * SCALE + b1,
+                s = jnp.concatenate(
+                    [s[:BLK] * SCALE + bias[row:row + 1, :], s[BLK:] * SCALE + bias[row + 1:row + 2, :]], axis=0
                 )
+                peak = jnp.max(s, axis=1, keepdims=True)
                 if slot == SELF:
-                    new = jnp.maximum(peak, FLOOR)
+                    new = jnp.broadcast_to(peak, (2 * BLK, DH))
                 else:
-                    old = top[who, head, 0:1, :]
+                    old = top[who, head]
                     new = jnp.maximum(old, peak)
-                p = jnp.concatenate(
-                    [jnp.exp2(s0 * SCALE - (new - b0)), jnp.exp2(s1 * SCALE - (new - b1))], axis=0
-                )
-                part = jnp.sum(p.reshape(2 * BLK // 8, 8, 2 * BLK), axis=0)
-                mixed = lax.dot_general(
-                    v, p.astype(jnp.bfloat16), (((0,), (0,)), ((), ())), preferred_element_type=jnp.float32
-                )
+                p = jnp.exp2(s - jnp.concatenate([new, new], axis=1))
+                part = p[:, :DH] + p[:, DH:]
+                mixed = jnp.dot(p.astype(jnp.bfloat16), v, preferred_element_type=jnp.float32)
                 if slot != SELF:
                     rescale = jnp.exp2(old - new)
                     part = part + total[who, head] * rescale
                     mixed = mixed + acc[who, head] * rescale
-                top[who, head, 0:1, :] = new
+                top[who, head] = new
                 total[who, head] = part
                 acc[who, head] = mixed
 
     def pack_guest(j):
+        lane = lax.broadcasted_iota(jnp.int32, (2 * BLK, DH), 1)
+        table = jnp.zeros((2 * BLK, DH), jnp.float32)
         for hh in range(PER):
             head = j * PER + hh
-            guest_out[j, hh * DH:(hh + 1) * DH, :] = acc[1, head].astype(jnp.bfloat16)
-            guest_stat[j, 2 * hh:2 * hh + 1, :] = top[1, head, 0:1, :]
-            guest_stat[j, 2 * hh + 1:2 * hh + 2, :] = jnp.sum(total[1, head], axis=0, keepdims=True)
+            guest_out[j, :, hh * DH:(hh + 1) * DH] = acc[1, head].astype(jnp.bfloat16)
+            denom = jnp.sum(total[1, head], axis=1, keepdims=True)
+            table = jnp.where(lane == 2 * hh, top[1, head], table)
+            table = jnp.where(lane == 2 * hh + 1, denom, table)
+        guest_stat[j] = table.T[:8]
 
     def finish(j):
+        table = jnp.concatenate([back_stat[j]] * (DH // 8), axis=0).T
         for hh in range(PER):
             head = j * PER + hh
-            m1, m2 = top[0, head, 0:1, :], back_stat[j, 2 * hh:2 * hh + 1, :]
+            m1, m2 = top[0, head], table[:, 2 * hh:2 * hh + 1]
             m = jnp.maximum(m1, m2)
             e1, e2 = jnp.exp2(m1 - m), jnp.exp2(m2 - m)
-            l1 = jnp.sum(total[0, head], axis=0, keepdims=True)
-            denom = l1 * e1 + back_stat[j, 2 * hh + 1:2 * hh + 2, :] * e2
-            other = back_out[j, hh * DH:(hh + 1) * DH, :].astype(jnp.float32)
-            mixed = acc[0, head] * (e1 / denom) + other * (e2 / denom)
+            l1 = jnp.sum(total[0, head], axis=1, keepdims=True)
+            denom = l1 * e1 + table[:, 2 * hh + 1:2 * hh + 2] * e2
+            other = back_out[j, :, hh * DH:(hh + 1) * DH].astype(jnp.float32)
             cols = pl.ds(pl.multiple_of(head * DH, DH), DH)
-            o_ref[:, cols] = mixed.T.astype(jnp.bfloat16)
+            o_ref[:, cols] = ((acc[0, head] * e1 + other * e2) / denom).astype(jnp.bfloat16)
 
     def launch(j):
         own_copy(j, 0).wait()
@@ -297,12 +292,12 @@
             pltpu.VMEM((2, CHUNKS, rows, HALF), jnp.bfloat16),
             pltpu.VMEM((BIAS_ROWS, rows), jnp.float32),
             pltpu.VMEM((SLOTS, CHUNKS, rows, 2 * HALF), jnp.bfloat16),
-            pltpu.VMEM((2, HEADS, DH, rows), jnp.float32),
-            pltpu.VMEM((2, HEADS, 8, rows), jnp.float32),
-            pltpu.VMEM((2, HEADS, 8, rows), jnp.float32),
-            pltpu.VMEM((CHUNKS, HALF, rows), jnp.bfloat16),
+            pltpu.VMEM((2, HEADS, rows, DH), jnp.float32),
+            pltpu.VMEM((2, HEADS, rows, DH), jnp.float32),
+            pltpu.VMEM((2, HEADS, rows, DH), jnp.float32),
+            pltpu.VMEM((CHUNKS, rows, HALF), jnp.bfloat16),
             pltpu.VMEM((CHUNKS, 8, rows), jnp.float32),
-            pltpu.VMEM((CHUNKS, HALF, rows), jnp.bfloat16),
+            pltpu.VMEM((CHUNKS, rows, HALF), jnp.bfloat16),
             pltpu.VMEM((CHUNKS, 8, rows), jnp.float32),
             pltpu.SemaphoreType.DMA((CHUNKS, 3)),
             pltpu.SemaphoreType.DMA((9, CHUNKS)),

time: 71.3 us -> 66.9 us (0.938)
  Pallas kernels: 69 us -> 64.6 us
    pallas_call x1, Pallas kernels: 69 us -> 64.6 us  [shards(): pl.pallas_call(kernel, out_shape=jax.ShapeDtypeStruct((rows, width), jnp....]
where the time goes in v2:
time: 66.9 us; the launch traced here: 66.6 us
  Pallas kernels  64.6 us (97%)
  local copies, waits for them, and re-layouts  2.06 us (3%)
    pallas_call x1, Pallas kernels, shards(): pl.pallas_call(kernel, out_shape=jax.ShapeDtypeStruct((rows, width), jnp....  64.6 us
    unnamed x1, local copies, waits for them, and re-layouts  2.06 us

profile of v2, /device:TPU:17, one launch (start us, length us, event | category | flops | bytes accessed | tf_op | source)
XLA Modules:
  0.0 66.6 jit_solution(16408010491647425845)
XLA Ops:
  0.0 64.6 %shard_map.46 = bf16[256,1536]{1,0:T(8,128)(2,1)} custom-call(bf16[256,1536]{1,0:T(8,128)(2,1)} %q_hbm.1, bf16[256,1536]{1,0:T(8,128)(2,1)} %k_hbm.1, bf16[256,1536]{1,0:T(8,128)(2,1)} %v_hbm.1, s32[26,64]{1,0:T(8,128)} %bitcast.1), custom_call_target="tpu_custom_call" | custom-call | tf_op jit(solution)/shard_map/pallas_call | solution.py:286
  64.6 2.1 %copy.6 = bf16[256,1536]{1,0:T(8,128)(2,1)} copy(bf16[256,1536]{1,0:T(8,128)(2,1)} %shard_map.46) | data formatting | bytes 1572864
